TPU v7x, 768 devices: a whole 4x8x12 slice. The times are simulated.
768 devices in a mesh: tm: 8 (over z_hi, x), row: 16 (over y, core), col: 6 (over z_lo).
Axes of the slice: x: 4, y: 8, z: 12 (z_hi: 2, z_lo: 6; z = z_hi * 6 + z_lo), core: 2. Of those that a mesh axis runs over, the one named last changes fastest.
Arguments:
- c_occ: float32 [1536, 1536], P(None, 'tm'), may hold values from -1 to 1
- c_vir: float32 [1536, 1536], P(None, 'tm'), may hold values from -1 to 1
- eps_occ: float32 [1536], P('tm'), may hold values from -1.6 to -0.05, as said below
- eps_vir: float32 [1536], P('tm'), may hold values from 0.05 to 1.6, as said below
- tau: float32 [8], replicated, may hold values from 0.03 to 10
- tweight: float32 [8], replicated, may hold values from 0.02 to 0.15
- omega: float32 [32], replicated, may hold values from 0.05 to 5
- coulomb: float32 [1536, 1536], replicated, may hold values from -2 to 2
Outputs:
- screened: float32 [32, 1536, 1536], P('tm', 'row', 'col')
Inputs may be any that keep to these rules, and one draw needn't show every extreme that they name: `eps_occ`: ascending along the orbital index. `eps_vir`: ascending along the orbital index.
All inputs are finite; a program needn't handle non-finite values.
Results may differ from a plain program's by a relative error of at most 0.00005.
Values sent between devices are 32-bit elements; how exact they have to be, the bound alone decides.
A program may use at most 64 MiB of HBM per device.

v0:
```python
import jax
import jax.numpy as jnp
from jax import lax
from jax.sharding import Mesh
from jax.sharding import PartitionSpec as P

TM = ("tm_0", "tm_1")


HIGH = lax.Precision.HIGHEST


def own_block(parts, axes, order):
    inside = parts.shape[1:]
    parts = parts.reshape(*(lax.axis_size(a) for a in axes), *inside)
    parts = jnp.moveaxis(parts, order, range(len(axes))).reshape(-1, *inside)
    for k in order:
        parts = lax.psum_scatter(parts, axes[k], scatter_dimension=0, tiled=True)
    return parts[0]


def in_blocks(value, dim, peers):
    before, after = (value.shape[:dim], value.shape[dim + 1 :])
    return jnp.moveaxis(value.reshape(*before, peers, -1, *after), dim, 0)


def sum_by_axis(value, axes, order, dim):
    peers = lax.axis_size(axes)
    return own_block(in_blocks(value, dim, peers), axes, order)


def copy_for_each(value, axis):
    copies = jnp.broadcast_to(value, (lax.axis_size(axis), *value.shape))
    return lax.all_to_all(copies, axis, split_axis=0, concat_axis=0, tiled=True)


def laid_out(parts, dim):
    dims = list(parts.shape[1:])
    dims[dim] *= parts.shape[0]
    return jnp.moveaxis(parts, 0, dim).reshape(dims)


def gathered_copies(value, axis, dim):
    parts = copy_for_each(value, axis)
    return laid_out(parts, dim)


def green_block(rows_c, cols_c, energies, taus, sign):
    factor = jnp.exp(sign * taus[:, None] * energies[None, :])
    width = rows_c.shape[1]
    scaled = rows_c[:, None, :] * factor[None, :, :]
    lead = (rows_c.shape[0], taus.shape[0])
    flat = scaled.reshape(lead[0] * lead[1], width)
    product = lax.dot_general(
        flat, cols_c, (((1,), (1,)), ((), ())), precision=HIGH, preferred_element_type=jnp.float32
    )
    return product.reshape(lead[0], lead[1], cols_c.shape[0])


def on_device(c_occ, c_vir, eps_occ, eps_vir, tau, tweight, omega, coulomb):
    grid = coulomb.shape[0]
    tile_rows = grid // lax.axis_size("row")
    tile_cols = grid // lax.axis_size("col")
    row_start = lax.axis_index("row") * tile_rows
    col_start = lax.axis_index("col") * tile_cols
    occ_rows = lax.dynamic_slice_in_dim(c_occ, row_start, tile_rows, 0)
    occ_cols = lax.dynamic_slice_in_dim(c_occ, col_start, tile_cols, 0)
    vir_rows = lax.dynamic_slice_in_dim(c_vir, row_start, tile_rows, 0)
    vir_cols = lax.dynamic_slice_in_dim(c_vir, col_start, tile_cols, 0)
    gamma = tweight[None, :] * jnp.cos(omega[:, None] * tau[None, :])
    green_occ = green_block(occ_rows, occ_cols, eps_occ, tau, 1.0)
    green_vir = green_block(vir_rows, vir_cols, eps_vir, tau, -1.0)
    greens = sum_by_axis(jnp.stack([green_occ, green_vir], axis=1), TM, (1, 0), 0)
    polar_time = -2.0 * greens[:, 0] * greens[:, 1]
    polar_all = jnp.einsum("kj,ijc->kic", gamma, polar_time, precision=HIGH)
    polar = lax.all_to_all(polar_all, TM, split_axis=0, concat_axis=1, tiled=True)
    coulomb_rows = lax.dynamic_slice_in_dim(coulomb, row_start, tile_rows, 0)
    coulomb_cols = lax.dynamic_slice_in_dim(coulomb, col_start, tile_cols, 1)
    coulomb_tile = lax.dynamic_slice_in_dim(coulomb_rows, col_start, tile_cols, 1)
    left = coulomb_rows
    coupled = jnp.einsum(
        "ik,fkj->fij", left, lax.all_gather(polar, "row", axis=1, tiled=True), precision=HIGH
    )
    coupled_rows = gathered_copies(coupled, "col", 2)
    first = coulomb_tile[None] + jnp.einsum(
        "fik,kj->fij", coupled_rows, coulomb_cols, precision=HIGH
    )
    left = coupled_rows
    return jnp.einsum(
        "fik,fkj->fij", left, lax.all_gather(first, "row", axis=1, tiled=True), precision=HIGH
    )


def solution(mesh):
    split = Mesh(
        mesh.devices.reshape(2, 4, mesh.shape["row"], mesh.shape["col"]),
        ("tm_0", "tm_1", "row", "col"),
    )
    placed = (P(None, TM), P(None, TM), P(TM), P(TM), P(), P(), P(), P())
    return jax.shard_map(
        on_device, mesh=split, in_specs=placed, out_specs=P(TM, "row", "col"), check_vma=False
    )
```

profile of v0, /device:TPU:1, one launch (start us, length us, event | category | flops | bytes accessed | tf_op | source)
XLA Modules:
  0.0 340.0 jit_solution(14913981994231732464)
XLA Ops:
  6.5 0.7 broadcast_multiply_fusion
  7.2 0.8 multiply_exponential_fusion.1
  7.9 1.1 constant_dynamic-slice_fusion
  9.3 0.8 multiply_exponential_fusion
  10.0 1.7 fusion.8
  11.8 1.7 fusion.6
  13.7 1.3 copy.20
  15.0 40.5 %reduce-scatter.3.cloned.1.call-done = f32[2,12,2,8,256]{4,3,1,2,0:T(8,128)} async-done(((f32[8,12,2,8,256]{4,3,1,2,0:T(8,128)}), f32[2,12,2,8,256]{4,3,1,2,0:T(8,128)}) %reduce-scatter.3.cloned.1.call-update) | async-done | bytes 393232 | tf_op jit(solution)/shard_map/reduce_scatter | solution.py:18
  55.6 43.3 %reduce-scatter.5.cloned.1.call-done = f32[1,12,2,8,256]{4,3,1,2,0:T(8,128)} async-done(((f32[2,12,2,8,256]{4,3,1,2,0:T(8,128)}), f32[1,12,2,8,256]{4,3,1,2,0:T(8,128)}) %reduce-scatter.5.cloned.1.call-update) | async-done | bytes 196624 | tf_op jit(solution)/shard_map/reduce_scatter | solution.py:18
  98.9 1.6 fusion.21
  100.7 19.0 %all_to_all.23 = f32[32,12,256]{2,1,0:T(8,128)S(1)} all-to-all(f32[32,12,256]{2,1,0:T(8,128)S(1)} %copy.21), channel_id=1, replica_groups=mesh['tm_0'=2,'tm_1'=4,'row'=16,'col'=6] {'tm_0','tm_1'}, dimensions={0} | all-to-all | bytes 786432 | tf_op jit(solution)/shard_map/all_to_all | solution.py:76
  119.6 0.3 copy.22
  119.9 0.8 copy.23
  120.7 57.0 %all-gather.3.cloned.1.call-done = f32[4,1536,256]{2,1,0:T(8,128)} async-done(((f32[4,96,256]{2,1,0:T(8,128)}), f32[4,1536,256]{2,1,0:T(8,128)}) %all-gather.3.cloned.1.call-update) | async-done | bytes 6291472 | tf_op jit(solution)/shard_map/all_gather | solution.py:82
  177.7 6.1 %convolution_bitcast_fusion = f32[4,96,256]{2,1,0:T(8,128)S(1)} fusion(f32[4,1536,256]{2,1,0:T(8,128)} %all-gather.3.cloned.1.call-done, f32[1536,1536]{1,0:T(8,128)} %param.15, s32[]{:T(128)S(6)} %select_n.15), kind=kOutput, calls=%fused_computation.5 | convolution fusion | flops 1811939328 | bytes 7274500 | tf_op jit(solution)/shard_map/ik,fkj->fij/dot_general | solution.py:81
  183.8 1.7 broadcast_in_dim.2
  185.5 8.2 %all-to-all-start.1 = ((f32[6,4,96,256]{3,2,1,0:T(8,128)}), f32[6,4,96,256]{3,2,1,0:T(8,128)S(1)}, u32[]{:S(2)}, u32[]{:S(2)}) async-start(f32[6,4,96,256]{3,2,1,0:T(8,128)} %broadcast_in_dim.2), calls=%async_computation.3 | async-start | bytes 4718592 | tf_op jit(solution)/shard_map/all_to_all | solution.py:34
  193.7 1.0 dynamic_slice.26
  194.7 72.3 %all-to-all-done.1 = f32[6,4,96,256]{3,2,1,0:T(8,128)S(1)} async-done(((f32[6,4,96,256]{3,2,1,0:T(8,128)}), f32[6,4,96,256]{3,2,1,0:T(8,128)S(1)}, u32[]{:S(2)}, u32[]{:S(2)}) %all-to-all-start.1) | async-done | bytes 2359328 | tf_op jit(solution)/shard_map/all_to_all | solution.py:34
  267.0 1.4 copy-done
  268.4 2.0 copy.25
  270.4 4.2 %fusion.3 = f32[4,96,256]{2,1,0:T(8,128)} fusion(f32[4,96,1536]{2,1,0:T(8,128)S(1)} %bitcast.39, f32[1536,1536]{1,0:T(8,128)} %param.15, s32[]{:T(128)S(6)} %select_n.16, f32[96,256]{1,0:T(8,128)S(1)} %dynamic_slice.26), kind=kOutput, calls=%fused_computation.4 | convolution fusion | flops 1812037632 | bytes 4423684 | tf_op jit(solution)/shard_map/fik,kj->fij/dot_general | solution.py:85
  274.6 51.4 %all-gather.5.cloned.1.call-done = f32[4,1536,256]{2,1,0:T(8,128)} async-done(((f32[4,96,256]{2,1,0:T(8,128)}), f32[4,1536,256]{2,1,0:T(8,128)}) %all-gather.5.cloned.1.call-update) | async-done | bytes 6291472 | tf_op jit(solution)/shard_map/all_gather | solution.py:90
  326.0 7.4 %fusion.36 = f32[4,96,256]{2,1,0:T(8,128)} fusion(f32[4,96,1536]{2,1,0:T(8,128)S(1)} %bitcast.40, f32[4,1536,256]{2,1,0:T(8,128)} %all-gather.5.cloned.1.call-done), kind=kOutput, calls=%fused_computation.42 | convolution fusion | flops 1811939328 | bytes 9043968 | tf_op jit(solution)/shard_map/fik,fkj->fij/dot_general | solution.py:89
  (19 shorter events, 0.7 us)
Async XLA Ops:
  6.5 49.0 %reduce-scatter.3.cloned.1.call-start = ((), (), s32[]{:S(2)}) async-start(), calls=%async_computation.4 | async-start | bytes 1966080 | tf_op jit(solution)/shard_map/reduce_scatter | solution.py:18
  13.6 85.2 %copy-start.1 = (f32[8]{0:T(128)S(1)}, f32[8]{0:T(128)}, u32[]{:S(2)}) copy-start(f32[8]{0:T(128)} %param.12) | copy-start | bytes 100
  13.6 85.2 %copy-start.2 = (f32[32]{0:T(128)S(1)}, f32[32]{0:T(128)}, u32[]{:S(2)}) copy-start(f32[32]{0:T(128)} %param.14) | copy-start | bytes 388
  13.6 85.2 %copy-start.3 = (f32[8]{0:T(128)S(1)}, f32[8]{0:T(128)}, u32[]{:S(2)}) copy-start(f32[8]{0:T(128)} %param.13) | copy-start | bytes 100
  15.0 83.9 %reduce-scatter.5.cloned.1.call-start = ((), (), s32[]{:S(2)}) async-start(), calls=%async_computation.5 | async-start | bytes 589824 | tf_op jit(solution)/shard_map/reduce_scatter | solution.py:18
  55.5 122.2 %all-gather.3.cloned.1.call-start = ((), (), s32[]{:S(2)}) async-start(), calls=%async_computation.6 | async-start | bytes 6684672 | tf_op jit(solution)/shard_map/all_gather | solution.py:82
  185.5 81.5 %all-to-all-start.1 = ((f32[6,4,96,256]{3,2,1,0:T(8,128)}), f32[6,4,96,256]{3,2,1,0:T(8,128)S(1)}, u32[]{:S(2)}, u32[]{:S(2)}) async-start(f32[6,4,96,256]{3,2,1,0:T(8,128)} %broadcast_in_dim.2), calls=%async_computation.3 | async-start | bytes 4718592 | tf_op jit(solution)/shard_map/all_to_all | solution.py:34
  193.7 132.3 %all-gather.5.cloned.1.call-start = ((), (), s32[]{:S(2)}) async-start(), calls=%async_computation.7 | async-start | bytes 6684672 | tf_op jit(solution)/shard_map/all_gather | solution.py:90
  267.0 1.4 copy-start
Sparse Core Ops, SparseCore 0:
  15.1 40.3 reduce-scatter.2
  58.6 40.2 reduce-scatter.4
  120.9 56.8 all-gather.2
  274.8 51.1 all-gather.4
where the time goes:
time: 340 us
  waiting for transfers between devices  264 us (78%)
  matrix products  22.7 us (7%)
  blocking collectives  19 us (6%)
  between operations  13.2 us (4%)
  local copies, waits for them, and re-layouts  10 us (3%)
  starting transfers between devices  8.25 us (2%)
    reduce_scatter x2, waiting for transfers between devices, own_block(): parts = lax.psum_scatter(parts, axes[k], scatter_dimension=0, tiled=True)  83.7 us
    all_to_all x1, waiting for transfers between devices, copy_for_each(): return lax.all_to_all(copies, axis, split_axis=0, concat_axis=0, tiled=True)  72.3 us
    all_gather x1, waiting for transfers between devices, on_device(): lax.all_gather(polar, 'row', axis=1, tiled=True)  57 us
    all_gather x1, waiting for transfers between devices, on_device(): lax.all_gather(first, 'row', axis=1, tiled=True)  51.4 us
    all_to_all x1, blocking collectives, on_device(): lax.all_to_all(polar_all, TM, split_axis=0, concat_axis=1, tiled=True)  19 us
    all_to_all x1, starting transfers between devices, copy_for_each(): return lax.all_to_all(copies, axis, split_axis=0, concat_axis=0, tiled=True)  8.17 us
    dot_general x1, matrix products, on_device(): jnp.einsum('fik,fkj->fij', left, lax.all_gather(first, 'row', axis=1, til...  7.44 us
  transfers between devices with their start and end apart: 5, of which 5 were waited for; matrix products, arithmetic and copies ran while one was open for 0% of the time, Pallas kernels for 0%

commit v1 on v0

v1 whole, which is shorter than its diff:
```python
import jax
import jax.numpy as jnp
from jax import lax
from jax.experimental import pallas as pl
from jax.experimental.pallas import tpu as pltpu
from jax.sharding import Mesh
from jax.sharding import PartitionSpec as P

AXES = ("zh", "x", "y", "c", "zl")
MESH_ID = pl.DeviceIdType.MESH
F32, BF16 = jnp.float32, jnp.bfloat16


def halves(value):
    high = value.astype(BF16)
    return high, (value - high.astype(F32)).astype(BF16)


def dot(a, b):
    return lax.dot_general(a, b, (((1,), (0,)), ((), ())), preferred_element_type=F32)


def remote(src, dst, send, recv, device):
    return pltpu.make_async_remote_copy(
        src_ref=src, dst_ref=dst, send_sem=send, recv_sem=recv, device_id=device, device_id_type=MESH_ID
    )


def kernel(
    tau, gamma, eps_occ, eps_vir, occ, vir, coulomb, out,
    rows_t, left, part, half_in, from_side, z_out, z_in, times, freqs, blocks,
    p_high, p_low, v_full, v_high, v_low, first, stack_a, stack_b, tiles, landed,
    v_sem, x_send, x_recv, z_send, z_recv, a_send, a_self, a_recv,
    l_send, l_recv, y_send, y_recv, c_send, c_recv, o_send, o_recv,
):
    zh, x, y, c, zl = (lax.axis_index(a) for a in AXES)
    level = zl + zh * (5 - 2 * zl)
    own = level * 2 + c
    parity = lax.rem(y, 2)
    pair = lax.div(y, 2)
    x_right, x_left = lax.rem(x + 1, 4), lax.rem(x + 3, 4)
    other = 1 - zh

    def at(zh_=zh, x_=x, y_=y, c_=c, zl_=zl):
        return (zh_, x_, y_, c_, zl_)

    def line_of(zh_, level_):
        return level_ + zh_ * (5 - 2 * level_)

    load_v = pltpu.make_async_copy(coulomb, v_full, v_sem)
    load_v.start()

    barrier = pltpu.get_barrier_semaphore()

    def greet(device):
        pl.semaphore_signal(barrier, inc=1, device_id=device, device_id_type=MESH_ID)

    turn = 6 * (2 * parity + c) + zl + 6 * pair + 15
    strip = lax.rem(turn, 24)

    def tile_to(col, h):
        half = 2 * strip + h
        q = lax.div(half, 3)
        return q, lax.rem(half, 3), jnp.logical_and(q == 2 * y + c, col == zl)

    def tile_from(f, slot):
        r = lax.div(3 * (2 * y + c) + slot, 2)
        u = lax.rem(r + 48 - 15 - 6 * f, 24)
        pc, zl_s = lax.div(u, 6), lax.rem(u, 6)
        y_s, c_s = 2 * f + lax.div(pc, 2), lax.rem(pc, 2)
        same = jnp.logical_and(jnp.logical_and(y_s == y, c_s == c), zl_s == zl)
        return at(y_=y_s, c_=c_s, zl_=zl_s), same

    def freq_to(k):
        zh_k, x_k, f = lax.div(k, 16), lax.rem(lax.div(k, 4), 4), lax.rem(k, 4)
        y_k = 2 * f + lax.rem(x, 2)
        same = jnp.logical_and(jnp.logical_and(zh_k == zh, x_k == x), y_k == y)
        return (zh_k, x_k, y_k, c, line_of(zh_k, level)), same

    greet(at(x_=x_left))
    greet(at(x_=x_right))
    greet(at(zh_=other, zl_=5 - zl))
    greet(at(y_=y + 1 - 2 * parity))
    greet(at(c_=1 - c))

    @pl.when(zl > 0)
    def _():
        greet(at(zl_=zl - 1))

    @pl.when(zl < 5)
    def _():
        greet(at(zl_=zl + 1))

    def greet_source(n, carry):
        zh_s, x_s, y_s = lax.div(n, 16), 2 * lax.rem(lax.div(n, 8), 2) + parity, lax.rem(n, 8)
        same = jnp.logical_and(jnp.logical_and(zh_s == zh, x_s == x), y_s == y)

        @pl.when(jnp.logical_not(same))
        def _():
            greet((zh_s, x_s, y_s, c, line_of(zh_s, level)))

        return carry

    lax.fori_loop(0, 32, greet_source, 0)

    def greet_tile(n, carry):
        device, same = tile_from(lax.div(n, 3), lax.rem(n, 3))

        @pl.when(jnp.logical_not(same))
        def _():
            greet(device)

        return carry

    lax.fori_loop(0, 12, greet_tile, 0)

    for side, (block, eps, sign) in enumerate(((occ, eps_occ, 1.0), (vir, eps_vir, -1.0))):
        rows_t[...] = block[:, pl.ds(pl.multiple_of(own * 128, 128), 128)].T
        rows = rows_t[pl.ds(pl.multiple_of(y * 16, 16), 16), :]
        for t in range(8):
            high, low = halves(rows * jnp.exp(eps[...] * (sign * tau[t])))
            left[side, t * 16 : t * 16 + 16, :] = high
            left[side, 128 + t * 16 : 144 + t * 16, :] = low
    for d in (2, 1, 3, 0):
        for z in range(2):
            col = lax.rem(own + z * 4 + lax.rem(x + d, 4), 12)
            for side, block in enumerate((occ, vir)):
                high, low = halves(block[:, pl.ds(pl.multiple_of(col * 128, 128), 128)])
                both = dot(left[side], high)
                part[d, z, side * 128 : side * 128 + 128, :] = (
                    both[:128] + both[128:] + dot(left[side, :128, :], low)
                )

    is_self = jnp.logical_and(lax.rem(x, 2) == parity, True).astype(jnp.int32)
    tile_self = jnp.int32(0)
    for h in range(2):
        tile_self = tile_self + (tile_to(zl, h)[2]).astype(jnp.int32)
    inner = (zl > 0).astype(jnp.int32) + (zl < 5).astype(jnp.int32)
    pl.semaphore_wait(barrier, 5 + inner + 32 - is_self + 12 - tile_self)

    right_dev, left_dev = at(x_=x_right), at(x_=x_left)
    sends = [
        remote(part.at[2, 0], half_in.at[0], x_send.at[0], x_recv.at[0], right_dev),
        remote(part.at[2, 1], half_in.at[1], x_send.at[1], x_recv.at[1], left_dev),
        remote(part.at[1, 1], from_side.at[0, 1], x_send.at[2], x_recv.at[2], right_dev),
        remote(part.at[3, 0], from_side.at[1, 0], x_send.at[3], x_recv.at[3], left_dev),
        remote(part.at[1, 0], from_side.at[0, 0], x_send.at[4], x_recv.at[4], right_dev),
        remote(part.at[3, 1], from_side.at[1, 1], x_send.at[5], x_recv.at[5], left_dev),
    ]
    for n in range(4):
        sends[n].start()
    sends[0].wait_recv()
    part[1, 0] = part[1, 0] + half_in[0]
    sends[4].start()
    sends[1].wait_recv()
    part[3, 1] = part[3, 1] + half_in[1]
    sends[5].start()

    load_v.wait()

    def split_v(n, carry):
        rows = pl.ds(pl.multiple_of(n * 64, 64), 64)
        high, low = halves(v_full[rows, :])
        v_high[rows, :] = high
        v_low[rows, :] = low
        return carry

    lax.fori_loop(0, 24, split_v, 0)
    for n in range(2, 6):
        sends[n].wait_recv()

    z_out[...] = part[0, other] + from_side[0, other] + from_side[1, other]
    cross = remote(z_out, z_in, z_send, z_recv, at(zh_=other, zl_=5 - zl))
    cross.start()
    z_keep = part[0, zh] + from_side[0, zh] + from_side[1, zh]
    half_in[0] = z_keep
    cross.wait_recv()
    times[...] = -2.0 * (half_in[0, :128, :] + z_in[:128, :]) * (half_in[0, 128:, :] + z_in[128:, :])

    def one_freq(k, carry):
        total = gamma[k, 0] * times[0:16, :]
        for t in range(1, 8):
            total = total + gamma[k, t] * times[t * 16 : t * 16 + 16, :]
        freqs[k] = total
        return carry

    lax.fori_loop(0, 32, one_freq, 0)

    member = zh * 4 + x
    place = blocks.at[own, lax.rem(x, 2), lax.div(member, 2), pl.ds(pl.multiple_of(y * 16, 16), 16), :]
    mine = member * 4 + pair

    def send_freq(n, carry):
        k = lax.rem(mine + n, 32)
        device, _same = freq_to(k)
        remote(freqs.at[k], place, a_send, a_recv, device).start()
        return carry

    lax.fori_loop(1, 32, send_freq, 0)
    to_pair, same_pair = freq_to(mine)

    @pl.when(same_pair)
    def _():
        pltpu.make_async_copy(freqs.at[mine], place, a_recv).start()

    @pl.when(jnp.logical_not(same_pair))
    def _():
        remote(freqs.at[mine], place, a_self, a_recv, to_pair).start()

    own_block = blocks.at[own, parity]
    pltpu.make_async_copy(own_block, own_block, a_recv).wait()

    def needed(level_, par, m2):
        return jnp.logical_or(m2 < 3, jnp.logical_and(par == 0, level_ < 3))

    def expand(i, par, m2):
        m = 2 * m2 + par
        col = lax.rem(i + m, 12)
        here = pl.ds(pl.multiple_of(i * 128, 128), 128)
        there = pl.ds(pl.multiple_of(col * 128, 128), 128)
        value = blocks[i, par, m2]
        high, low = halves(value)
        p_high[here, there] = high
        p_low[here, there] = low

        @pl.when(m > 0)
        def _():
            high_t, low_t = halves(value.T)
            p_high[there, here] = high_t
            p_low[there, here] = low_t

    def line_copy(j, m2, side):
        ref = blocks.at[line_of(zh, j) * 2 + c, parity, m2]
        return remote(ref, ref, l_send.at[side, j * 4 + m2], l_recv.at[j * 4 + m2], at(zl_=zl + 1 - 2 * side))

    def y_copy(j, m2, par):
        ref = blocks.at[line_of(zh, j) * 2 + c, par, m2]
        return remote(ref, ref, y_send.at[j * 4 + m2], y_recv.at[j * 4 + m2], at(y_=y + 1 - 2 * parity))

    def c_copy(j, m2, par, core):
        ref = blocks.at[line_of(zh, j) * 2 + core, par, m2]
        n = par * 24 + j * 4 + m2
        return remote(ref, ref, c_send.at[n], c_recv.at[n], at(c_=1 - c))

    def from_line(j, m2, d, side):
        copy = line_copy(j, m2, side)

        @pl.when(d > 0)
        def _():
            copy.wait_recv()

        far = zl + 1 - 2 * side

        @pl.when(jnp.logical_and(far >= 0, far < 6))
        def _():
            copy.start()

        @pl.when(jnp.logical_or(d > 0, side == 0))
        def _():
            y_copy(j, m2, parity).start()
            c_copy(j, m2, parity, c).start()
            expand(line_of(zh, j) * 2 + c, parity, m2)

    def from_pair(j, m2):
        y_copy(j, m2, 1 - parity).wait_recv()
        c_copy(j, m2, 1 - parity, c).start()
        expand(line_of(zh, j) * 2 + c, 1 - parity, m2)

    def from_core(j, m2, par):
        c_copy(j, m2, par, 1 - c).wait_recv()
        expand(line_of(zh, j) * 2 + 1 - c, par, m2)

    def gather(n, carry):
        step, m2, side = lax.div(n, 8), lax.rem(lax.div(n, 2), 4), lax.rem(n, 2)

        def stage(lag, par, action, twice=False):
            d = step - lag
            j = zl - d * (1 - 2 * side)
            live = jnp.logical_and(jnp.logical_and(d >= 0, d < 6), jnp.logical_and(j >= 0, j < 6))
            if not twice:
                live = jnp.logical_and(live, jnp.logical_or(d > 0, side == 0))
            live = jnp.logical_and(live, needed(line_of(zh, j), par, m2))

            @pl.when(live)
            def _():
                action(j, d)

        stage(0, parity, lambda j, d: from_line(j, m2, d, side), True)
        stage(1, 1 - parity, lambda j, d: from_pair(j, m2))
        stage(1, parity, lambda j, d: from_core(j, m2, parity))
        stage(2, 1 - parity, lambda j, d: from_core(j, m2, 1 - parity))
        return carry

    lax.fori_loop(0, 64, gather, 0)

    rows = pl.ds(pl.multiple_of(strip * 64, 64), 64)
    stack_a[:64, :] = v_high[rows, :]
    stack_a[64:, :] = v_low[rows, :]

    def product(src, high, low, use):
        def step(n, carry):
            cols = pl.ds(pl.multiple_of(n * 256, 256), 256)
            both = dot(src[...], high[:, cols])
            use(n, cols, both[:64] + both[64:] + dot(src[:64, :], low[:, cols]))
            return carry

        lax.fori_loop(0, 6, step, 0)

    def keep(dst, cols, value):
        high, low = halves(value)
        dst[:64, cols] = high
        dst[64:, cols] = low

    def use_one(n, cols, value):
        first[:, cols] = value
        keep(stack_b, cols, value)

    def send_tile(n, cols, value):
        tiles[n] = value
        for h in range(2):
            q, slot, same = tile_to(n, h)
            src = tiles.at[n, pl.ds(32 * h, 32), :]
            dst = landed.at[pair, slot]

            @pl.when(same)
            def _():
                pltpu.make_async_copy(src, dst, o_recv).start()

            @pl.when(jnp.logical_not(same))
            def _():
                remote(src, dst, o_send.at[2 * n + h], o_recv, at(y_=lax.div(q, 2), c_=lax.rem(q, 2), zl_=n)).start()

    product(stack_a, p_high, p_low, use_one)
    product(stack_b, v_high, v_low, lambda n, cols, value: keep(stack_a, cols, value))
    product(stack_a, p_high, p_low, lambda n, cols, value: keep(stack_b, cols, first[:, cols] + value))
    product(stack_b, v_high, v_low, send_tile)

    pltpu.make_async_copy(landed, landed, o_recv).wait()
    out[...] = landed[...].reshape(out.shape)

    for n in range(6):
        sends[n].wait_send()
    cross.wait_send()
    pltpu.make_async_copy(freqs.at[pl.ds(0, 31)], freqs.at[pl.ds(0, 31)], a_send).wait()

    @pl.when(jnp.logical_not(same_pair))
    def _():
        pltpu.make_async_copy(freqs.at[0], freqs.at[0], a_self).wait()

    def drain(n, carry):
        j, m2 = lax.div(n, 4), lax.rem(n, 4)
        level_ = line_of(zh, j)

        @pl.when(needed(level_, parity, m2))
        def _():
            y_copy(j, m2, parity).wait_send()
            c_copy(j, m2, parity, c).wait_send()

            @pl.when(jnp.logical_and(j <= zl, zl < 5))
            def _():
                line_copy(j, m2, 0).wait_send()

            @pl.when(jnp.logical_and(j >= zl, zl > 0))
            def _():
                line_copy(j, m2, 1).wait_send()

        @pl.when(needed(level_, 1 - parity, m2))
        def _():
            c_copy(j, m2, 1 - parity, c).wait_send()

        return carry

    lax.fori_loop(0, 24, drain, 0)

    def drain_tiles(n, carry):
        col, h = lax.div(n, 2), lax.rem(n, 2)
        same = tile_to(col, h)[2]

        @pl.when(jnp.logical_not(same))
        def _():
            src = tiles.at[0, pl.ds(0, 32), :]
            pltpu.make_async_copy(src, src, o_send.at[n]).wait()

        return carry

    lax.fori_loop(0, 12, drain_tiles, 0)


def on_device(c_occ, c_vir, eps_occ, eps_vir, tau, tweight, omega, coulomb):
    gamma = tweight[None, :] * jnp.cos(omega[:, None] * tau[None, :])
    grid = coulomb.shape[0]
    width = c_occ.shape[1]
    dma = pltpu.SemaphoreType.DMA
    vmem, smem = pl.BlockSpec(memory_space=pltpu.VMEM), pl.BlockSpec(memory_space=pltpu.SMEM)
    return pl.pallas_call(
        kernel,
        out_shape=jax.ShapeDtypeStruct((4, 96, 256), F32),
        in_specs=[smem, smem, vmem, vmem, vmem, vmem, pl.BlockSpec(memory_space=pl.ANY)],
        out_specs=vmem,
        scratch_shapes=[
            pltpu.VMEM((128, width), F32),
            pltpu.VMEM((2, 256, width), BF16),
            pltpu.VMEM((4, 2, 256, 128), F32),
            pltpu.VMEM((2, 256, 128), F32),
            pltpu.VMEM((2, 2, 256, 128), F32),
            pltpu.VMEM((256, 128), F32),
            pltpu.VMEM((256, 128), F32),
            pltpu.VMEM((128, 128), F32),
            pltpu.VMEM((32, 16, 128), F32),
            pltpu.VMEM((12, 2, 4, 128, 128), F32),
            pltpu.VMEM((grid, grid), BF16),
            pltpu.VMEM((grid, grid), BF16),
            pltpu.VMEM((grid, grid), F32),
            pltpu.VMEM((grid, grid), BF16),
            pltpu.VMEM((grid, grid), BF16),
            pltpu.VMEM((64, grid), F32),
            pltpu.VMEM((128, grid), BF16),
            pltpu.VMEM((128, grid), BF16),
            pltpu.VMEM((6, 64, 256), F32),
            pltpu.VMEM((4, 3, 32, 256), F32),
            dma, dma((6,)), dma((6,)), dma, dma, dma, dma, dma,
            dma((2, 24)), dma((24,)), dma((24,)), dma((24,)), dma((48,)), dma((48,)), dma((12,)), dma,
        ],
        compiler_params=pltpu.CompilerParams(
            collective_id=0, has_side_effects=True, vmem_limit_bytes=60 * 1024 * 1024
        ),
        name="screened",
    )(tau, gamma, eps_occ[None, :], eps_vir[None, :], c_occ.T, c_vir.T, coulomb)


def solution(mesh):
    split = Mesh(mesh.devices.reshape(2, 4, 8, 2, 6), AXES)
    tm = ("zh", "x")
    placed = (P(None, tm), P(None, tm), P(tm), P(tm), P(), P(), P(), P())
    return jax.shard_map(
        on_device, mesh=split, in_specs=placed, out_specs=P(tm, ("y", "c"), "zl"), check_vma=False
    )
```

time: 340 us -> 114 us (0.34)
  waiting for transfers between devices: 264 us -> 0 us
  Pallas kernels: 0 us -> 109 us
  matrix products: 22.7 us -> 0 us
  blocking collectives: 19 us -> 0 us
  between operations: 13.2 us -> 0.01 us
  starting transfers between devices: 8.25 us -> 0 us
  local copies, waits for them, and re-layouts: 10 us -> 1.77 us
    pallas_call x0 -> x1, Pallas kernels: none -> 109 us  [on_device(): pl.pallas_call(kernel, out_shape=jax.ShapeDtypeStruct((4, 96, 256), F32),...]
    all_gather x2 -> x0, waiting for transfers between devices: 108 us -> none  [the longest x1 57 us: on_device(): lax.all_gather(polar, 'row', axis=1, tiled=True)]
    reduce_scatter x2 -> x0, waiting for transfers between devices: 83.7 us -> none  [own_block(): parts = lax.psum_scatter(parts, axes[k], scatter_dimension=0, tiled=True)]
    all_to_all x1 -> x0, waiting for transfers between devices: 72.3 us -> none  [copy_for_each(): return lax.all_to_all(copies, axis, split_axis=0, concat_axis=0, tiled=True)]
    dot_general x6 -> x0, matrix products: 22.7 us -> none  [the longest x1 7.44 us: on_device(): jnp.einsum('fik,fkj->fij', left, lax.all_gather(first, 'row', axis=1, til...]
    all_to_all x1 -> x0, blocking collectives: 19 us -> none  [on_device(): lax.all_to_all(polar_all, TM, split_axis=0, concat_axis=1, tiled=True)]
    all_to_all x1 -> x0, starting transfers between devices: 8.17 us -> none  [copy_for_each(): return lax.all_to_all(copies, axis, split_axis=0, concat_axis=0, tiled=True)]
  transfers between devices with their start and end apart: 5 -> 0, of which waited for: 5 -> 0; matrix products, arithmetic and copies ran while one was open for 0% -> 0% of each run, Pallas kernels for 0% -> 0%
where the time goes in v1:
time: 114 us; the launch traced here: 112 us
  Pallas kernels  109 us (96%)
  local copies, waits for them, and re-layouts  1.77 us (2%)
  other arithmetic  1.43 us (1%)
    pallas_call x1, Pallas kernels, on_device(): pl.pallas_call(kernel, out_shape=jax.ShapeDtypeStruct((4, 96, 256), F32),...  109 us

profile of v1, /device:TPU:1, one launch (start us, length us, event | category | flops | bytes accessed | tf_op | source)
XLA Modules:
  0.0 112.2 jit_solution(4077759011501513357)
XLA Ops:
  0.0 1.4 %cosine_multiply_fusion.gamma = f32[32,8]{1,0:T(8,128)} fusion(f32[8]{0:T(128)} %param.13, f32[8]{0:T(128)} %tau.1, f32[32]{0:T(128)} %param.14), kind=kLoop, calls=%fused_computation | loop fusion | flops 512 | bytes 1216 | tf_op jit(solution)/shard_map/mul | solution.py:390
  1.4 109.0 %screened.1 = f32[4,96,256]{2,1,0:T(8,128)} custom-call(f32[8]{0:T(128)} %tau.1, f32[32,8]{1,0:T(8,128)} %cosine_multiply_fusion.gamma, f32[1,192]{1,0:T(1,128)} %bitcast.6, f32[1,192]{1,0:T(1,128)} %bitcast.7, f32[192,1536]{1,0:T(8,128)} %bitcast.4, f32[192,1536]{1,0:T(8,128)} %bitcast.5, f32[1536,1536]{1,0:T(8,128)} %coulomb.1), custom_call_target="tpu_custom_call" | custom-call | tf_op jit(solution)/shard_map/screened/pallas_call | solution.py:395
  110.5 1.8 %copy.11 = f32[4,96,256]{2,1,0:T(8,128)} copy(f32[4,96,256]{2,1,0:T(8,128)} %screened.1) | data formatting | bytes 786432

commit v2 on v1

v2 whole, which is shorter than its diff:
```python
import jax
import jax.numpy as jnp
from jax import lax
from jax.experimental import pallas as pl
from jax.experimental.pallas import tpu as pltpu
from jax.sharding import Mesh
from jax.sharding import PartitionSpec as P

AXES = ("zh", "x", "y", "c", "zl")
MESH_ID = pl.DeviceIdType.MESH
F32, BF16 = jnp.float32, jnp.bfloat16

BATCH = 4
SPREAD = ("xyz", "zxy", "zyx", "xyz")
PIECES = (
    (0, 0, 0, 0), (1, 0, 0, 0), (2, 0, 0, 0), (3, 0, 0, 0), (0, 0, 1, 0), (0, 0, 0, 1),
    (0, 1, 0, 0), (1, 1, 0, 0), (1, 0, 1, 0), (1, 0, 0, 1), (2, 1, 0, 0), (2, 0, 0, 1),
    (2, 0, 1, 0), (0, 2, 0, 0), (3, 0, 1, 0), (3, 0, 0, 1), (3, 1, 0, 0), (0, 0, 1, 1),
    (1, 1, 1, 0), (0, 1, 1, 0), (0, 1, 0, 1), (1, 2, 0, 0), (1, 1, 0, 1), (1, 0, 1, 1),
    (2, 1, 1, 0), (2, 0, 1, 1), (2, 2, 0, 0), (2, 1, 0, 1), (3, 2, 0, 0), (1, 2, 1, 0),
    (3, 1, 1, 0), (3, 1, 0, 1), (3, 0, 1, 1), (1, 2, 0, 1), (0, 2, 1, 0), (0, 2, 0, 1),
    (1, 1, 1, 1), (0, 1, 1, 1), (2, 2, 1, 0), (2, 1, 1, 1), (2, 2, 0, 1), (3, 2, 1, 0),
    (3, 2, 0, 1), (0, 2, 1, 1), (1, 2, 1, 1), (3, 1, 1, 1), (2, 2, 1, 1), (3, 2, 1, 1),
)


def halves(value):
    high = value.astype(BF16)
    return high, (value - high.astype(F32)).astype(BF16)


def dot(a, b):
    return lax.dot_general(a, b, (((1,), (0,)), ((), ())), preferred_element_type=F32)


def remote(src, dst, send, recv, device):
    return pltpu.make_async_remote_copy(
        src_ref=src, dst_ref=dst, send_sem=send, recv_sem=recv, device_id=device, device_id_type=MESH_ID
    )


def kernel(
    tau, tweight, omega, eps_occ, eps_vir, occ_in, vir_in, coulomb, out,
    rows_t, left, part, half_in, from_side, z_out, z_in, times, freqs, blocks,
    p_high, p_low, v_full, v_high, v_low, first, stack_a, stack_b, tiles, landed,
    tables, occ, vir, b_sem, v_sem, x_send, x_recv, z_send, z_recv, a_send, a_self, a_recv,
    g_send, g_recv, c_send, c_recv, o_send, o_recv,
):
    zh, x, y, c, zl = (lax.axis_index(a) for a in AXES)
    level = zl + zh * (5 - 2 * zl)
    own = level * 2 + c
    triple, bz = lax.div(level, 3), lax.rem(level, 3)
    x_pair, bx = lax.div(x, 2), lax.rem(x, 2)
    y_pair, by = lax.div(y, 2), lax.rem(y, 2)
    x_freq = 2 * x_pair + lax.rem(y_pair, 2)
    slot_freq = 2 * lax.div(y_pair, 2) + triple
    home = (by * 3 + bz) * 2 + c
    x_right, x_left = lax.rem(x + 1, 4), lax.rem(x + 3, 4)
    other = 1 - zh

    def at(zh_=zh, x_=x, y_=y, c_=c, zl_=zl):
        return (zh_, x_, y_, c_, zl_)

    def line_of(zh_, level_):
        return level_ + zh_ * (5 - 2 * level_)

    load_v = pltpu.make_async_copy(coulomb, v_full, v_sem)
    loads = [
        pltpu.make_async_copy(occ_in, occ, b_sem.at[0]),
        pltpu.make_async_copy(vir_in, vir, b_sem.at[1]),
    ]
    for load in loads:
        load.start()
    load_v.start()

    barrier = pltpu.get_barrier_semaphore()

    def greet(device):
        pl.semaphore_signal(barrier, inc=1, device_id=device, device_id_type=MESH_ID)

    strip = lax.rem(6 * (2 * by + bx) + c * 3 + bz + 6 * y_pair + 15, 24)

    def tile_to(col, h):
        half = 2 * strip + h
        q = lax.div(half, 3)
        same = jnp.logical_and(jnp.logical_and(q == 2 * y + c, col == zl), x_freq == x)
        return q, lax.rem(half, 3), same

    def tile_from(f, slot):
        y_pair_s = 2 * lax.div(f, 2) + bx
        r = lax.div(3 * (2 * y + c) + slot, 2)
        u = lax.rem(r + 81 - 6 * y_pair_s, 24)
        a, b = lax.div(u, 6), lax.rem(u, 6)
        x_s, y_s = 2 * x_pair + lax.rem(a, 2), 2 * y_pair_s + lax.div(a, 2)
        zl_s, c_s = line_of(zh, 3 * lax.rem(f, 2) + lax.rem(b, 3)), lax.div(b, 3)
        same = jnp.logical_and(
            jnp.logical_and(y_s == y, c_s == c), jnp.logical_and(zl_s == zl, x_s == x)
        )
        return at(x_=x_s, y_=y_s, c_=c_s, zl_=zl_s), same

    def freq_to(k):
        zh_k, x_k, f = lax.div(k, 16), lax.rem(lax.div(k, 4), 4), lax.rem(k, 4)
        x_d = 2 * lax.div(x_k, 2) + bx
        y_d = 2 * (2 * lax.div(f, 2) + lax.rem(x_k, 2)) + triple
        return (zh_k, x_d, y_d, c, line_of(zh_k, 3 * lax.rem(f, 2) + bz))

    greet(at(x_=x_left))
    greet(at(x_=x_right))
    greet(at(zh_=other, zl_=5 - zl))
    greet(at(y_=y + 1 - 2 * by))
    greet(at(c_=1 - c))

    def neighbour(step):
        return at(zl_=line_of(zh, level + step))

    @pl.when(bz > 0)
    def _():
        greet(neighbour(-1))

    @pl.when(bz < 2)
    def _():
        greet(neighbour(1))

    same_home = triple == by

    def greet_source(n, carry):
        zh_s, x_s, y_s = lax.div(n, 16), 2 * lax.rem(lax.div(n, 8), 2) + bx, lax.rem(n, 8)
        same = jnp.logical_and(jnp.logical_and(zh_s == zh, x_s == x), y_s == y)

        @pl.when(jnp.logical_not(jnp.logical_and(same, same_home)))
        def _():
            greet((zh_s, x_s, y_s, c, line_of(zh_s, by * 3 + bz)))

        return carry

    lax.fori_loop(0, 32, greet_source, 0)

    def greet_tile(n, carry):
        device, same = tile_from(lax.div(n, 3), lax.rem(n, 3))

        @pl.when(jnp.logical_not(same))
        def _():
            greet(device)

        return carry

    lax.fori_loop(0, 12, greet_tile, 0)

    for load in loads:
        load.wait()
    for side, (block, eps, sign) in enumerate(((occ, eps_occ, 1.0), (vir, eps_vir, -1.0))):
        rows_t[...] = block[:, pl.ds(pl.multiple_of(own * 128, 128), 128)].T
        rows = rows_t[pl.ds(pl.multiple_of(y * 16, 16), 16), :]
        for t in range(8):
            high, low = halves(rows * jnp.exp(eps[...] * (sign * tau[t])))
            left[side, t * 16 : t * 16 + 16, :] = high
            left[side, 128 + t * 16 : 144 + t * 16, :] = low

    def partial_sums(d):
        for z in range(2):
            col = lax.rem(own + z * 4 + lax.rem(x + d, 4), 12)
            for side, block in enumerate((occ, vir)):
                high, low = halves(block[:, pl.ds(pl.multiple_of(col * 128, 128), 128)])
                both = dot(left[side], high)
                part[d, z, side * 128 : side * 128 + 128, :] = (
                    both[:128] + both[128:] + dot(left[side, :128, :], low)
                )

    partial_sums(2)
    is_self = same_home.astype(jnp.int32)
    tile_self = jnp.int32(0)
    for h in range(2):
        tile_self = tile_self + (tile_to(zl, h)[2]).astype(jnp.int32)
    inner = (bz > 0).astype(jnp.int32) + (bz < 2).astype(jnp.int32)
    pl.semaphore_wait(barrier, 5 + inner + 32 - is_self + 12 - tile_self)

    right_dev, left_dev = at(x_=x_right), at(x_=x_left)
    sends = [
        remote(part.at[2, 0], half_in.at[0], x_send.at[0], x_recv.at[0], right_dev),
        remote(part.at[2, 1], half_in.at[1], x_send.at[1], x_recv.at[1], left_dev),
        remote(part.at[1, 1], from_side.at[0, 1], x_send.at[2], x_recv.at[2], right_dev),
        remote(part.at[3, 0], from_side.at[1, 0], x_send.at[3], x_recv.at[3], left_dev),
        remote(part.at[1, 0], from_side.at[0, 0], x_send.at[4], x_recv.at[4], right_dev),
        remote(part.at[3, 1], from_side.at[1, 1], x_send.at[5], x_recv.at[5], left_dev),
    ]
    sends[0].start()
    sends[1].start()
    partial_sums(1)
    partial_sums(3)
    sends[2].start()
    sends[3].start()
    partial_sums(0)
    sends[0].wait_recv()
    part[1, 0] = part[1, 0] + half_in[0]
    sends[4].start()
    sends[1].wait_recv()
    part[3, 1] = part[3, 1] + half_in[1]
    sends[5].start()

    load_v.wait()

    def split_v(n, carry):
        rows = pl.ds(pl.multiple_of(n * 64, 64), 64)
        high, low = halves(v_full[rows, :])
        v_high[rows, :] = high
        v_low[rows, :] = low
        return carry

    lax.fori_loop(0, 24, split_v, 0)
    for t in range(8):
        tables[t : t + 1, :] = jnp.cos(omega[...] * tau[t]) * tweight[t]
    for n in range(2, 6):
        sends[n].wait_recv()

    z_out[...] = part[0, other] + from_side[0, other] + from_side[1, other]
    cross = remote(z_out, z_in, z_send, z_recv, at(zh_=other, zl_=5 - zl))
    cross.start()
    z_keep = part[0, zh] + from_side[0, zh] + from_side[1, zh]
    half_in[0] = z_keep
    cross.wait_recv()
    times[...] = -2.0 * (half_in[0, :128, :] + z_in[:128, :]) * (half_in[0, 128:, :] + z_in[128:, :])

    table = tables[...]
    for k in range(32):
        total = table[0:1, k : k + 1] * times[0:16, :]
        for t in range(1, 8):
            total = total + table[t : t + 1, k : k + 1] * times[t * 16 : t * 16 + 16, :]
        freqs[k] = total

    member = zh * 4 + x
    place = blocks.at[own, bx, lax.div(member, 2), pl.ds(pl.multiple_of(y * 16, 16), 16), :]
    mine = (zh * 4 + x_freq) * 4 + slot_freq

    def send_freq(n, carry):
        k = lax.rem(mine + n, 32)
        remote(freqs.at[k], place, a_send, a_recv, freq_to(k)).start()
        return carry

    lax.fori_loop(1, 32, send_freq, 0)

    @pl.when(same_home)
    def _():
        pltpu.make_async_copy(freqs.at[mine], place, a_recv).start()

    @pl.when(jnp.logical_not(same_home))
    def _():
        remote(freqs.at[mine], place, a_self, a_recv, freq_to(mine)).start()

    own_block = blocks.at[home, bx]
    pltpu.make_async_copy(own_block, own_block, a_recv).wait()

    def expand(i, par, m2):
        m = 2 * m2 + par
        col = lax.rem(i + m, 12)
        here = pl.ds(pl.multiple_of(i * 128, 128), 128)
        there = pl.ds(pl.multiple_of(col * 128, 128), 128)
        value = blocks[i, par, m2]
        high, low = halves(value)
        p_high[here, there] = high
        p_low[here, there] = low

        @pl.when(m > 0)
        def _():
            high_t, low_t = halves(value.T)
            p_high[there, here] = high_t
            p_low[there, here] = low_t

    others = (bz, jnp.where(bz == 1, 0, 1), jnp.where(bz == 2, 0, 2))
    pair_devices = {"x": at(x_=x + 1 - 2 * bx), "y": at(y_=y + 1 - 2 * by)}
    middle = bz == 1
    up, down = 1, -1

    def source(piece, core):
        m2, ez, ex, ey = piece
        par = bx if ex == 0 else 1 - bx
        side = by if ey == 0 else 1 - by
        i = (side * 3 + others[ez]) * 2 + core
        live = None if m2 < 3 else jnp.logical_and(par == 0, side == 0)
        return i, par, live

    def guarded(live, action):
        if live is None:
            action()
        else:
            pl.when(live)(action)

    def copy_of(n, piece, lane, device):
        i, par, _live = source(piece, c)
        ref = blocks.at[i, par, piece[0]]
        return remote(ref, ref, g_send.at[lane, n], g_recv.at[n_of(piece)], device)

    def n_of(piece):
        m2, ez, ex, ey = piece
        par = bx if ex == 0 else 1 - bx
        side = by if ey == 0 else 1 - by
        return ((m2 * 2 + side) * 2 + par) * 3 + others[ez]

    def core_copy(piece, core):
        i, par, _live = source(piece, core)
        ref = blocks.at[i, par, piece[0]]
        n = n_of(piece)
        return remote(ref, ref, c_send.at[n], c_recv.at[n], at(c_=1 - c))

    def arrival(piece):
        m2, ez, ex, ey = piece
        moved = {"z": ez, "x": ex, "y": ey}
        return max((p for p, d in enumerate(SPREAD[m2]) if moved[d]), default=-1)

    def sends_of(n, piece):
        m2, ez, _ex, _ey = piece
        last = arrival(piece)
        found = []
        for axis in SPREAD[m2][last + 1 :]:
            if axis == "z":
                found.append((bz < 2, copy_of(n, piece, 0, neighbour(up))))
                found.append((bz > 0, copy_of(n, piece, 1, neighbour(down))))
            else:
                found.append((None, copy_of(n, piece, 2 if axis == "x" else 3, pair_devices[axis])))
        if last >= 0 and SPREAD[m2][last] == "z":
            lane, step = (0, up) if ez == 1 else (1, down)
            found.append((middle, copy_of(n, piece, lane, neighbour(step))))
        return found

    def pick(values, q):
        found = values[-1]
        for at_q in range(len(values) - 2, -1, -1):
            found = jnp.where(q == at_q, values[at_q], found)
        return found

    def unfold(batch, cores):
        def step(q, carry):
            index = pick([t[0] for t in batch], q)
            ex, ey = pick([t[2] for t in batch], q), pick([t[3] for t in batch], q)
            sz = pick([others[t[1]] for t in batch], q)
            theirs = pick(cores, q)
            par, side = bx + ex - 2 * bx * ex, by + ey - 2 * by * ey
            core = c + theirs - 2 * c * theirs
            i = (side * 3 + sz) * 2 + core

            @pl.when(jnp.logical_or(index < 3, jnp.logical_and(par == 0, side == 0)))
            def _():
                @pl.when(theirs == 1)
                def _():
                    ref = blocks.at[i, par, index]
                    n = ((index * 2 + side) * 2 + par) * 3 + sz
                    remote(ref, ref, c_send.at[n], c_recv.at[n], at(c_=1 - c)).wait_recv()

                expand(i, par, index)

            return carry

        lax.fori_loop(0, len(batch), step, 0)

    batches = [PIECES[n : n + BATCH] for n in range(0, len(PIECES), BATCH)]
    for b in range(len(batches) + 1):
        if b < len(batches):
            for q, piece in enumerate(batches[b]):
                _i, _par, live = source(piece, c)

                def take(n=b * BATCH + q, piece=piece):
                    if arrival(piece) >= 0:
                        copy_of(n, piece, 0, neighbour(up)).wait_recv()
                    for when, copy in sends_of(n, piece):
                        guarded(when, copy.start)
                    core_copy(piece, c).start()

                guarded(live, take)
        mine_now = batches[b] if b < len(batches) else ()
        theirs_now = batches[b - 1] if b else ()
        unfold(mine_now + theirs_now, [0] * len(mine_now) + [1] * len(theirs_now))

    rows = pl.ds(pl.multiple_of(strip * 64, 64), 64)
    stack_a[:64, :] = v_high[rows, :]
    stack_a[64:, :] = v_low[rows, :]

    def product(src, high, low, use):
        def step(n, carry):
            cols = pl.ds(pl.multiple_of(n * 256, 256), 256)
            both = dot(src[...], high[:, cols])
            use(n, cols, both[:64] + both[64:] + dot(src[:64, :], low[:, cols]))
            return carry

        lax.fori_loop(0, 6, step, 0)

    def keep(dst, cols, value):
        high, low = halves(value)
        dst[:64, cols] = high
        dst[64:, cols] = low

    def use_one(n, cols, value):
        first[:, cols] = value
        keep(stack_b, cols, value)

    def send_tile(n, cols, value):
        tiles[n] = value
        for h in range(2):
            q, slot, same = tile_to(n, h)
            src = tiles.at[n, pl.ds(32 * h, 32), :]
            dst = landed.at[slot_freq, slot]

            @pl.when(same)
            def _():
                pltpu.make_async_copy(src, dst, o_recv).start()

            @pl.when(jnp.logical_not(same))
            def _():
                remote(src, dst, o_send.at[2 * n + h], o_recv, at(x_=x_freq, y_=lax.div(q, 2), c_=lax.rem(q, 2), zl_=n)).start()

    product(stack_a, p_high, p_low, use_one)
    product(stack_b, v_high, v_low, lambda n, cols, value: keep(stack_a, cols, value))
    product(stack_a, p_high, p_low, lambda n, cols, value: keep(stack_b, cols, first[:, cols] + value))
    product(stack_b, v_high, v_low, send_tile)

    for n in range(6):
        sends[n].wait_send()
    cross.wait_send()
    pltpu.make_async_copy(freqs.at[pl.ds(0, 31)], freqs.at[pl.ds(0, 31)], a_send).wait()

    @pl.when(jnp.logical_not(same_home))
    def _():
        pltpu.make_async_copy(freqs.at[0], freqs.at[0], a_self).wait()

    for n, piece in enumerate(PIECES):
        _i, _par, live = source(piece, c)

        def drain(n=n, piece=piece):
            for when, copy in sends_of(n, piece):
                guarded(when, copy.wait_send)
            core_copy(piece, c).wait_send()

        guarded(live, drain)

    pltpu.make_async_copy(landed, landed, o_recv).wait()
    out[...] = landed[...].reshape(out.shape)

    def drain_tiles(n, carry):
        col, h = lax.div(n, 2), lax.rem(n, 2)
        same = tile_to(col, h)[2]

        @pl.when(jnp.logical_not(same))
        def _():
            src = tiles.at[0, pl.ds(0, 32), :]
            pltpu.make_async_copy(src, src, o_send.at[n]).wait()

        return carry

    lax.fori_loop(0, 12, drain_tiles, 0)


def on_device(c_occ, c_vir, eps_occ, eps_vir, tau, tweight, omega, coulomb):
    grid = coulomb.shape[0]
    width = c_occ.shape[1]
    dma = pltpu.SemaphoreType.DMA
    hbm = pl.BlockSpec(memory_space=pl.ANY)
    vmem, smem = pl.BlockSpec(memory_space=pltpu.VMEM), pl.BlockSpec(memory_space=pltpu.SMEM)
    return pl.pallas_call(
        kernel,
        out_shape=jax.ShapeDtypeStruct((4, 96, 256), F32),
        in_specs=[smem, smem, vmem, vmem, vmem, hbm, hbm, hbm],
        out_specs=vmem,
        scratch_shapes=[
            pltpu.VMEM((128, width), F32),
            pltpu.VMEM((2, 256, width), BF16),
            pltpu.VMEM((4, 2, 256, 128), F32),
            pltpu.VMEM((2, 256, 128), F32),
            pltpu.VMEM((2, 2, 256, 128), F32),
            pltpu.VMEM((256, 128), F32),
            pltpu.VMEM((256, 128), F32),
            pltpu.VMEM((128, 128), F32),
            pltpu.VMEM((32, 16, 128), F32),
            pltpu.VMEM((12, 2, 4, 128, 128), F32),
            pltpu.VMEM((grid, grid), BF16),
            pltpu.VMEM((grid, grid), BF16),
            pltpu.VMEM((grid, grid), F32),
            pltpu.VMEM((grid, grid), BF16),
            pltpu.VMEM((grid, grid), BF16),
            pltpu.VMEM((64, grid), F32),
            pltpu.VMEM((128, grid), BF16),
            pltpu.VMEM((128, grid), BF16),
            pltpu.VMEM((6, 64, 256), F32),
            pltpu.VMEM((4, 3, 32, 256), F32),
            pltpu.VMEM((8, omega.shape[0]), F32),
            pltpu.VMEM((width, grid), F32),
            pltpu.VMEM((width, grid), F32),
            dma((2,)), dma, dma((6,)), dma((6,)), dma, dma, dma, dma, dma,
            dma((4, 48)), dma((48,)), dma((48,)), dma((48,)), dma((12,)), dma,
        ],
        compiler_params=pltpu.CompilerParams(
            collective_id=0, has_side_effects=True, vmem_limit_bytes=60 * 1024 * 1024
        ),
        name="screened",
    )(tau, tweight, omega[None, :], eps_occ[None, :], eps_vir[None, :], c_occ.T, c_vir.T, coulomb)


def solution(mesh):
    split = Mesh(mesh.devices.reshape(2, 4, 8, 2, 6), AXES)
    tm = ("zh", "x")
    placed = (P(None, tm), P(None, tm), P(tm), P(tm), P(), P(), P(), P())
    return jax.shard_map(
        on_device, mesh=split, in_specs=placed, out_specs=P(tm, ("y", "c"), "zl"), check_vma=False
    )
```

time: 114 us -> 109 us (0.956)
  the two profiles are of different devices: /device:TPU:1 before, /device:TPU:4 now
where the time goes in v2:
time: 109 us
  Pallas kernels  107 us (98%)
  local copies, waits for them, and re-layouts  1.77 us (2%)
    pallas_call x1, Pallas kernels, on_device(): pl.pallas_call(kernel, out_shape=jax.ShapeDtypeStruct((4, 96, 256), F32),...  107 us

profile of v2, /device:TPU:4, one launch (start us, length us, event | category | flops | bytes accessed | tf_op | source)
XLA Modules:
  0.0 108.9 jit_solution(5868738280021078592)
XLA Ops:
  0.0 107.1 %screened.1 = f32[4,96,256]{2,1,0:T(8,128)} custom-call(f32[8]{0:T(128)} %tau.1, f32[8]{0:T(128)} %tweight.1, f32[1,32]{1,0:T(1,128)} %bitcast.9, f32[1,192]{1,0:T(1,128)} %bitcast.7, f32[1,192]{1,0:T(1,128)} %bitcast.8, f32[192,1536]{1,0:T(8,128)} %bitcast.5, f32[192,1536]{1,0:T(8,128)} %bitcast.6, f32[1536,1536]{1,0:T(8,128)} %coulomb.1), custom_call_target="tpu_custom_call" | custom-call | tf_op jit(solution)/shard_map/screened/pallas_call | solution.py:456
  107.1 1.8 %copy.10 = f32[4,96,256]{2,1,0:T(8,128)} copy(f32[4,96,256]{2,1,0:T(8,128)} %screened.1) | data formatting | bytes 786432

commit v3 on v2

--- a/solution.py
+++ b/solution.py
@@ -11,16 +11,16 @@
 F32, BF16 = jnp.float32, jnp.bfloat16
 
 BATCH = 4
-SPREAD = ("xyz", "zxy", "zyx", "xyz")
+SPREAD = ("xzy", "yzx", "zxy", "yzx")
 PIECES = (
-    (0, 0, 0, 0), (1, 0, 0, 0), (2, 0, 0, 0), (3, 0, 0, 0), (0, 0, 1, 0), (0, 0, 0, 1),
-    (0, 1, 0, 0), (1, 1, 0, 0), (1, 0, 1, 0), (1, 0, 0, 1), (2, 1, 0, 0), (2, 0, 0, 1),
-    (2, 0, 1, 0), (0, 2, 0, 0), (3, 0, 1, 0), (3, 0, 0, 1), (3, 1, 0, 0), (0, 0, 1, 1),
-    (1, 1, 1, 0), (0, 1, 1, 0), (0, 1, 0, 1), (1, 2, 0, 0), (1, 1, 0, 1), (1, 0, 1, 1),
-    (2, 1, 1, 0), (2, 0, 1, 1), (2, 2, 0, 0), (2, 1, 0, 1), (3, 2, 0, 0), (1, 2, 1, 0),
-    (3, 1, 1, 0), (3, 1, 0, 1), (3, 0, 1, 1), (1, 2, 0, 1), (0, 2, 1, 0), (0, 2, 0, 1),
-    (1, 1, 1, 1), (0, 1, 1, 1), (2, 2, 1, 0), (2, 1, 1, 1), (2, 2, 0, 1), (3, 2, 1, 0),
-    (3, 2, 0, 1), (0, 2, 1, 1), (1, 2, 1, 1), (3, 1, 1, 1), (2, 2, 1, 1), (3, 2, 1, 1),
+    (0, 0, 0, 0), (1, 0, 0, 0), (0, 0, 1, 0), (0, 1, 0, 0), (0, 0, 0, 1), (2, 0, 0, 0),
+    (3, 0, 0, 0), (1, 0, 0, 1), (1, 1, 0, 0), (1, 0, 1, 0), (0, 2, 0, 0), (0, 1, 1, 0),
+    (0, 1, 0, 1), (0, 0, 1, 1), (2, 0, 1, 0), (2, 1, 0, 0), (3, 0, 1, 0), (1, 2, 0, 0),
+    (2, 0, 0, 1), (1, 1, 1, 0), (1, 0, 1, 1), (3, 1, 0, 0), (0, 2, 1, 0), (1, 1, 0, 1),
+    (3, 0, 0, 1), (0, 2, 0, 1), (2, 1, 1, 0), (2, 2, 0, 0), (0, 1, 1, 1), (3, 2, 0, 0),
+    (2, 0, 1, 1), (1, 2, 1, 0), (3, 1, 1, 0), (1, 2, 0, 1), (3, 0, 1, 1), (1, 1, 1, 1),
+    (3, 1, 0, 1), (2, 1, 0, 1), (2, 2, 1, 0), (0, 2, 1, 1), (3, 2, 0, 1), (3, 2, 1, 0),
+    (2, 1, 1, 1), (2, 2, 0, 1), (1, 2, 1, 1), (3, 1, 1, 1), (3, 2, 1, 1), (2, 2, 1, 1),
 )
 
 
@@ -41,7 +41,7 @@
 
 def kernel(
     tau, tweight, omega, eps_occ, eps_vir, occ_in, vir_in, coulomb, out,
-    rows_t, left, part, half_in, from_side, z_out, z_in, times, freqs, blocks,
+    rows_t, left, part, half_in, from_side, z_out, z_in, z_keep, times, freqs, blocks,
     p_high, p_low, v_full, v_high, v_low, first, stack_a, stack_b, tiles, landed,
     tables, occ, vir, b_sem, v_sem, x_send, x_recv, z_send, z_recv, a_send, a_self, a_recv,
     g_send, g_recv, c_send, c_recv, o_send, o_recv,
@@ -153,8 +153,10 @@
         rows = rows_t[pl.ds(pl.multiple_of(y * 16, 16), 16), :]
         for t in range(8):
             high, low = halves(rows * jnp.exp(eps[...] * (sign * tau[t])))
-            left[side, t * 16 : t * 16 + 16, :] = high
-            left[side, 128 + t * 16 : 144 + t * 16, :] = low
+            for h in range(2):
+                at_row = h * 64 + t * 8
+                left[side, at_row : at_row + 8, :] = high[h * 8 : h * 8 + 8]
+                left[side, 128 + at_row : 136 + at_row, :] = low[h * 8 : h * 8 + 8]
 
     def partial_sums(d):
         for z in range(2):
@@ -162,9 +164,9 @@
             for side, block in enumerate((occ, vir)):
                 high, low = halves(block[:, pl.ds(pl.multiple_of(col * 128, 128), 128)])
                 both = dot(left[side], high)
-                part[d, z, side * 128 : side * 128 + 128, :] = (
-                    both[:128] + both[128:] + dot(left[side, :128, :], low)
-                )
+                whole = both[:128] + both[128:] + dot(left[side, :128, :], low)
+                for h in range(2):
+                    part[d, z, h, side * 64 : side * 64 + 64, :] = whole[h * 64 : h * 64 + 64]
 
     partial_sums(2)
     is_self = same_home.astype(jnp.int32)
@@ -175,27 +177,38 @@
     pl.semaphore_wait(barrier, 5 + inner + 32 - is_self + 12 - tile_self)
 
     right_dev, left_dev = at(x_=x_right), at(x_=x_left)
+
+    def ring(n, src, dst, device):
+        return [
+            remote(src.at[h], dst.at[h], x_send.at[n, h], x_recv.at[n, h], device) for h in range(2)
+        ]
+
     sends = [
-        remote(part.at[2, 0], half_in.at[0], x_send.at[0], x_recv.at[0], right_dev),
-        remote(part.at[2, 1], half_in.at[1], x_send.at[1], x_recv.at[1], left_dev),
-        remote(part.at[1, 1], from_side.at[0, 1], x_send.at[2], x_recv.at[2], right_dev),
-        remote(part.at[3, 0], from_side.at[1, 0], x_send.at[3], x_recv.at[3], left_dev),
-        remote(part.at[1, 0], from_side.at[0, 0], x_send.at[4], x_recv.at[4], right_dev),
-        remote(part.at[3, 1], from_side.at[1, 1], x_send.at[5], x_recv.at[5], left_dev),
+        ring(0, part.at[2, 0], half_in.at[0], right_dev),
+        ring(1, part.at[2, 1], half_in.at[1], left_dev),
+        ring(2, part.at[1, 1], from_side.at[0, 1], right_dev),
+        ring(3, part.at[3, 0], from_side.at[1, 0], left_dev),
+        ring(4, part.at[1, 0], from_side.at[0, 0], right_dev),
+        ring(5, part.at[3, 1], from_side.at[1, 1], left_dev),
     ]
-    sends[0].start()
-    sends[1].start()
+    for h in range(2):
+        sends[0][h].start()
+        sends[1][h].start()
     partial_sums(1)
     partial_sums(3)
-    sends[2].start()
-    sends[3].start()
-    partial_sums(0)
-    sends[0].wait_recv()
-    part[1, 0] = part[1, 0] + half_in[0]
-    sends[4].start()
-    sends[1].wait_recv()
-    part[3, 1] = part[3, 1] + half_in[1]
-    sends[5].start()
+    for h in range(2):
+        sends[2][h].start()
+        sends[3][h].start()
+        sends[0][h].wait_recv()
+        part[1, 0, h] = part[1, 0, h] + half_in[0, h]
+        sends[4][h].start()
+        sends[1][h].wait_recv()
+        part[3, 1, h] = part[3, 1, h] + half_in[1, h]
+        sends[5][h].start()
+        if h == 0:
+            partial_sums(0)
+    for t in range(8):
+        tables[t : t + 1, :] = jnp.cos(omega[...] * tau[t]) * tweight[t]
 
     load_v.wait()
 
@@ -207,47 +220,48 @@
         return carry
 
     lax.fori_loop(0, 24, split_v, 0)
-    for t in range(8):
-        tables[t : t + 1, :] = jnp.cos(omega[...] * tau[t]) * tweight[t]
-    for n in range(2, 6):
-        sends[n].wait_recv()
-
-    z_out[...] = part[0, other] + from_side[0, other] + from_side[1, other]
-    cross = remote(z_out, z_in, z_send, z_recv, at(zh_=other, zl_=5 - zl))
-    cross.start()
-    z_keep = part[0, zh] + from_side[0, zh] + from_side[1, zh]
-    half_in[0] = z_keep
-    cross.wait_recv()
-    times[...] = -2.0 * (half_in[0, :128, :] + z_in[:128, :]) * (half_in[0, 128:, :] + z_in[128:, :])
-
+
+    cross = [
+        remote(z_out.at[h], z_in.at[h], z_send.at[h], z_recv.at[h], at(zh_=other, zl_=5 - zl))
+        for h in range(2)
+    ]
+    for h in range(2):
+        for n in range(2, 6):
+            sends[n][h].wait_recv()
+        z_out[h] = part[0, other, h] + from_side[0, other, h] + from_side[1, other, h]
+        cross[h].start()
+        z_keep[h] = part[0, zh, h] + from_side[0, zh, h] + from_side[1, zh, h]
+
+    member = zh * 4 + x
+    mine = (zh * 4 + x_freq) * 4 + slot_freq
     table = tables[...]
-    for k in range(32):
-        total = table[0:1, k : k + 1] * times[0:16, :]
-        for t in range(1, 8):
-            total = total + table[t : t + 1, k : k + 1] * times[t * 16 : t * 16 + 16, :]
-        freqs[k] = total
-
-    member = zh * 4 + x
-    place = blocks.at[own, bx, lax.div(member, 2), pl.ds(pl.multiple_of(y * 16, 16), 16), :]
-    mine = (zh * 4 + x_freq) * 4 + slot_freq
-
-    def send_freq(n, carry):
-        k = lax.rem(mine + n, 32)
-        remote(freqs.at[k], place, a_send, a_recv, freq_to(k)).start()
-        return carry
-
-    lax.fori_loop(1, 32, send_freq, 0)
-
-    @pl.when(same_home)
-    def _():
-        pltpu.make_async_copy(freqs.at[mine], place, a_recv).start()
-
-    @pl.when(jnp.logical_not(same_home))
-    def _():
-        remote(freqs.at[mine], place, a_self, a_recv, freq_to(mine)).start()
-
-    own_block = blocks.at[home, bx]
-    pltpu.make_async_copy(own_block, own_block, a_recv).wait()
+    for h in range(2):
+        cross[h].wait_recv()
+        for t in range(8):
+            green = [z_keep[h, v * 64 + t * 8 : v * 64 + t * 8 + 8, :] for v in range(2)]
+            rest = [z_in[h, v * 64 + t * 8 : v * 64 + t * 8 + 8, :] for v in range(2)]
+            times[t] = -2.0 * (green[0] + rest[0]) * (green[1] + rest[1])
+        for k in range(32):
+            total = table[0:1, k : k + 1] * times[0]
+            for t in range(1, 8):
+                total = total + table[t : t + 1, k : k + 1] * times[t]
+            freqs[h, k] = total
+        place = blocks.at[own, bx, lax.div(member, 2), pl.ds(pl.multiple_of(y * 16 + h * 8, 8), 8), :]
+
+        def send_freq(n, carry, h=h, place=place):
+            k = lax.rem(mine + n, 32)
+            remote(freqs.at[h, k], place, a_send.at[h], a_recv.at[lax.div(member, 2)], freq_to(k)).start()
+            return carry
+
+        lax.fori_loop(1, 32, send_freq, 0)
+
+        @pl.when(same_home)
+        def _(h=h, place=place):
+            pltpu.make_async_copy(freqs.at[h, mine], place, a_recv.at[lax.div(member, 2)]).start()
+
+        @pl.when(jnp.logical_not(same_home))
+        def _(h=h, place=place):
+            remote(freqs.at[h, mine], place, a_self.at[h], a_recv.at[lax.div(member, 2)], freq_to(mine)).start()
 
     def expand(i, par, m2):
         m = 2 * m2 + par
@@ -270,12 +284,16 @@
     middle = bz == 1
     up, down = 1, -1
 
+    def quarter(q):
+        return lax.rem(q + 2 * zh, 4)
+
     def source(piece, core):
         m2, ez, ex, ey = piece
         par = bx if ex == 0 else 1 - bx
         side = by if ey == 0 else 1 - by
         i = (side * 3 + others[ez]) * 2 + core
-        live = None if m2 < 3 else jnp.logical_and(par == 0, side == 0)
+        small = jnp.logical_and(par == 0, side == 0)
+        live = None if m2 % 2 == 0 else jnp.logical_or(quarter(m2) < 3, small)
         return i, par, live
 
     def guarded(live, action):
@@ -286,18 +304,18 @@
 
     def copy_of(n, piece, lane, device):
         i, par, _live = source(piece, c)
-        ref = blocks.at[i, par, piece[0]]
+        ref = blocks.at[i, par, quarter(piece[0])]
         return remote(ref, ref, g_send.at[lane, n], g_recv.at[n_of(piece)], device)
 
     def n_of(piece):
         m2, ez, ex, ey = piece
         par = bx if ex == 0 else 1 - bx
         side = by if ey == 0 else 1 - by
-        return ((m2 * 2 + side) * 2 + par) * 3 + others[ez]
+        return ((quarter(m2) * 2 + side) * 2 + par) * 3 + others[ez]
 
     def core_copy(piece, core):
         i, par, _live = source(piece, core)
-        ref = blocks.at[i, par, piece[0]]
+        ref = blocks.at[i, par, quarter(piece[0])]
         n = n_of(piece)
         return remote(ref, ref, c_send.at[n], c_recv.at[n], at(c_=1 - c))
 
@@ -329,7 +347,7 @@
 
     def unfold(batch, cores):
         def step(q, carry):
-            index = pick([t[0] for t in batch], q)
+            index = quarter(pick([t[0] for t in batch], q))
             ex, ey = pick([t[2] for t in batch], q), pick([t[3] for t in batch], q)
             sz = pick([others[t[1]] for t in batch], q)
             theirs = pick(cores, q)
@@ -364,6 +382,9 @@
                         guarded(when, copy.start)
                     core_copy(piece, c).start()
 
+                if arrival(piece) < 0:
+                    ref = blocks.at[home, bx, quarter(piece[0])]
+                    pltpu.make_async_copy(ref, ref, a_recv.at[quarter(piece[0])]).wait()
                 guarded(live, take)
         mine_now = batches[b] if b < len(batches) else ()
         theirs_now = batches[b - 1] if b else ()
@@ -373,8 +394,9 @@
     stack_a[:64, :] = v_high[rows, :]
     stack_a[64:, :] = v_low[rows, :]
 
-    def product(src, high, low, use):
+    def product(src, high, low, use, start=0):
         def step(n, carry):
+            n = lax.rem(n + start, 6)
             cols = pl.ds(pl.multiple_of(n * 256, 256), 256)
             both = dot(src[...], high[:, cols])
             use(n, cols, both[:64] + both[64:] + dot(src[:64, :], low[:, cols]))
@@ -409,16 +431,18 @@
     product(stack_a, p_high, p_low, use_one)
     product(stack_b, v_high, v_low, lambda n, cols, value: keep(stack_a, cols, value))
     product(stack_a, p_high, p_low, lambda n, cols, value: keep(stack_b, cols, first[:, cols] + value))
-    product(stack_b, v_high, v_low, send_tile)
-
-    for n in range(6):
-        sends[n].wait_send()
-    cross.wait_send()
-    pltpu.make_async_copy(freqs.at[pl.ds(0, 31)], freqs.at[pl.ds(0, 31)], a_send).wait()
-
-    @pl.when(jnp.logical_not(same_home))
-    def _():
-        pltpu.make_async_copy(freqs.at[0], freqs.at[0], a_self).wait()
+    product(stack_b, v_high, v_low, send_tile, jnp.where(zl < 3, 3, 0))
+
+    for h in range(2):
+        for n in range(6):
+            sends[n][h].wait_send()
+        cross[h].wait_send()
+        sent = freqs.at[h, pl.ds(0, 31)]
+        pltpu.make_async_copy(sent, sent, a_send.at[h]).wait()
+
+        @pl.when(jnp.logical_not(same_home))
+        def _(h=h):
+            pltpu.make_async_copy(freqs.at[h, 0], freqs.at[h, 0], a_self.at[h]).wait()
 
     for n, piece in enumerate(PIECES):
         _i, _par, live = source(piece, c)
@@ -461,13 +485,14 @@
         scratch_shapes=[
             pltpu.VMEM((128, width), F32),
             pltpu.VMEM((2, 256, width), BF16),
-            pltpu.VMEM((4, 2, 256, 128), F32),
-            pltpu.VMEM((2, 256, 128), F32),
-            pltpu.VMEM((2, 2, 256, 128), F32),
-            pltpu.VMEM((256, 128), F32),
-            pltpu.VMEM((256, 128), F32),
-            pltpu.VMEM((128, 128), F32),
-            pltpu.VMEM((32, 16, 128), F32),
+            pltpu.VMEM((4, 2, 2, 128, 128), F32),
+            pltpu.VMEM((2, 2, 128, 128), F32),
+            pltpu.VMEM((2, 2, 2, 128, 128), F32),
+            pltpu.VMEM((2, 128, 128), F32),
+            pltpu.VMEM((2, 128, 128), F32),
+            pltpu.VMEM((2, 128, 128), F32),
+            pltpu.VMEM((8, 8, 128), F32),
+            pltpu.VMEM((2, 32, 8, 128), F32),
             pltpu.VMEM((12, 2, 4, 128, 128), F32),
             pltpu.VMEM((grid, grid), BF16),
             pltpu.VMEM((grid, grid), BF16),
@@ -482,7 +507,7 @@
             pltpu.VMEM((8, omega.shape[0]), F32),
             pltpu.VMEM((width, grid), F32),
             pltpu.VMEM((width, grid), F32),
-            dma((2,)), dma, dma((6,)), dma((6,)), dma, dma, dma, dma, dma,
+            dma((2,)), dma, dma((6, 2)), dma((6, 2)), dma((2,)), dma((2,)), dma((2,)), dma((2,)), dma((4,)),
             dma((4, 48)), dma((48,)), dma((48,)), dma((48,)), dma((12,)), dma,
         ],
         compiler_params=pltpu.CompilerParams(

time: 109 us -> 106 us (0.972)
  the two profiles are of different devices: /device:TPU:4 before, /device:TPU:1 now
where the time goes in v3:
time: 106 us; the launch traced here: 105 us
  Pallas kernels  103 us (97%)
  local copies, waits for them, and re-layouts  1.77 us (2%)
    pallas_call x1, Pallas kernels, on_device(): pl.pallas_call(kernel, out_shape=jax.ShapeDtypeStruct((4, 96, 256), F32),...  103 us

profile of v3, /device:TPU:1, one launch (start us, length us, event | category | flops | bytes accessed | tf_op | source)
XLA Modules:
  0.0 104.7 jit_solution(17476229283169593384)
XLA Ops:
  0.0 102.9 %screened.1 = f32[4,96,256]{2,1,0:T(8,128)} custom-call(f32[8]{0:T(128)} %tau.1, f32[8]{0:T(128)} %tweight.1, f32[1,32]{1,0:T(1,128)} %bitcast.9, f32[1,192]{1,0:T(1,128)} %bitcast.7, f32[1,192]{1,0:T(1,128)} %bitcast.8, f32[192,1536]{1,0:T(8,128)} %bitcast.5, f32[192,1536]{1,0:T(8,128)} %bitcast.6, f32[1536,1536]{1,0:T(8,128)} %coulomb.1), custom_call_target="tpu_custom_call" | custom-call | tf_op jit(solution)/shard_map/screened/pallas_call | solution.py:480
  102.9 1.8 %copy.10 = f32[4,96,256]{2,1,0:T(8,128)} copy(f32[4,96,256]{2,1,0:T(8,128)} %screened.1) | data formatting | bytes 786432

commit v4 on v3

--- a/solution.py
+++ b/solution.py
@@ -13,14 +13,14 @@
 BATCH = 4
 SPREAD = ("xzy", "yzx", "zxy", "yzx")
 PIECES = (
-    (0, 0, 0, 0), (1, 0, 0, 0), (0, 0, 1, 0), (0, 1, 0, 0), (0, 0, 0, 1), (2, 0, 0, 0),
-    (3, 0, 0, 0), (1, 0, 0, 1), (1, 1, 0, 0), (1, 0, 1, 0), (0, 2, 0, 0), (0, 1, 1, 0),
-    (0, 1, 0, 1), (0, 0, 1, 1), (2, 0, 1, 0), (2, 1, 0, 0), (3, 0, 1, 0), (1, 2, 0, 0),
-    (2, 0, 0, 1), (1, 1, 1, 0), (1, 0, 1, 1), (3, 1, 0, 0), (0, 2, 1, 0), (1, 1, 0, 1),
-    (3, 0, 0, 1), (0, 2, 0, 1), (2, 1, 1, 0), (2, 2, 0, 0), (0, 1, 1, 1), (3, 2, 0, 0),
-    (2, 0, 1, 1), (1, 2, 1, 0), (3, 1, 1, 0), (1, 2, 0, 1), (3, 0, 1, 1), (1, 1, 1, 1),
-    (3, 1, 0, 1), (2, 1, 0, 1), (2, 2, 1, 0), (0, 2, 1, 1), (3, 2, 0, 1), (3, 2, 1, 0),
-    (2, 1, 1, 1), (2, 2, 0, 1), (1, 2, 1, 1), (3, 1, 1, 1), (3, 2, 1, 1), (2, 2, 1, 1),
+    (0, 0, 0, 0), (1, 0, 0, 0), (0, 0, 1, 0), (2, 0, 0, 0), (1, 1, 0, 0), (3, 0, 0, 0),
+    (0, 1, 0, 0), (1, 0, 0, 1), (2, 0, 1, 0), (2, 1, 0, 0), (0, 0, 1, 1), (1, 2, 0, 0),
+    (3, 0, 0, 1), (1, 1, 1, 0), (3, 1, 0, 0), (0, 1, 1, 0), (0, 2, 0, 0), (0, 1, 0, 1),
+    (1, 1, 0, 1), (0, 0, 0, 1), (2, 0, 0, 1), (2, 2, 0, 0), (2, 0, 1, 1), (1, 0, 1, 0),
+    (3, 2, 0, 0), (2, 1, 1, 0), (3, 0, 1, 0), (1, 0, 1, 1), (0, 2, 1, 0), (3, 1, 0, 1),
+    (1, 2, 1, 0), (1, 2, 0, 1), (0, 2, 0, 1), (2, 2, 1, 0), (0, 1, 1, 1), (3, 2, 0, 1),
+    (3, 1, 1, 1), (3, 1, 1, 0), (2, 1, 1, 1), (2, 2, 0, 1), (3, 2, 1, 0), (1, 2, 1, 1),
+    (2, 1, 0, 1), (0, 2, 1, 1), (2, 2, 1, 1), (3, 0, 1, 1), (1, 1, 1, 1), (3, 2, 1, 1),
 )
 
 
@@ -479,7 +479,7 @@
     vmem, smem = pl.BlockSpec(memory_space=pltpu.VMEM), pl.BlockSpec(memory_space=pltpu.SMEM)
     return pl.pallas_call(
         kernel,
-        out_shape=jax.ShapeDtypeStruct((4, 96, 256), F32),
+        out_shape=pltpu.VMEM((4, 96, 256), F32),
         in_specs=[smem, smem, vmem, vmem, vmem, hbm, hbm, hbm],
         out_specs=vmem,
         scratch_shapes=[

time: 106 us -> 102 us (0.962)
  the two profiles are of different devices: /device:TPU:1 before, /device:TPU:128 now
where the time goes in v4:
time: 102 us
  Pallas kernels  101 us (99%)
    pallas_call x1, Pallas kernels, on_device(): pl.pallas_call(kernel, out_shape=pltpu.VMEM((4, 96, 256), F32), in_specs=...  101 us

profile of v4, /device:TPU:128, one launch (start us, length us, event | category | flops | bytes accessed | tf_op | source)
XLA Modules:
  0.0 102.0 jit_solution(10244435167554719052)
XLA Ops:
  0.0 101.3 %screened.1 = f32[4,96,256]{2,1,0:T(8,128)S(1)} custom-call(f32[8]{0:T(128)} %tau.1, f32[8]{0:T(128)} %tweight.1, f32[1,32]{1,0:T(1,128)} %bitcast.9, f32[1,192]{1,0:T(1,128)} %bitcast.7, f32[1,192]{1,0:T(1,128)} %bitcast.8, f32[192,1536]{1,0:T(8,128)} %bitcast.5, f32[192,1536]{1,0:T(8,128)} %bitcast.6, f32[1536,1536]{1,0:T(8,128)} %coulomb.1), custom_call_target="tpu_custom_call" | custom-call | tf_op jit(solution)/shard_map/screened/pallas_call | solution.py:480
  101.3 0.7 copy.10

commit v5 on v4

--- a/solution.py
+++ b/solution.py
@@ -10,17 +10,17 @@
 MESH_ID = pl.DeviceIdType.MESH
 F32, BF16 = jnp.float32, jnp.bfloat16
 
-BATCH = 4
+BATCHES = (4,) * 11 + (2, 1, 1)
 SPREAD = ("xzy", "yzx", "zxy", "yzx")
 PIECES = (
-    (0, 0, 0, 0), (1, 0, 0, 0), (0, 0, 1, 0), (2, 0, 0, 0), (1, 1, 0, 0), (3, 0, 0, 0),
-    (0, 1, 0, 0), (1, 0, 0, 1), (2, 0, 1, 0), (2, 1, 0, 0), (0, 0, 1, 1), (1, 2, 0, 0),
-    (3, 0, 0, 1), (1, 1, 1, 0), (3, 1, 0, 0), (0, 1, 1, 0), (0, 2, 0, 0), (0, 1, 0, 1),
-    (1, 1, 0, 1), (0, 0, 0, 1), (2, 0, 0, 1), (2, 2, 0, 0), (2, 0, 1, 1), (1, 0, 1, 0),
-    (3, 2, 0, 0), (2, 1, 1, 0), (3, 0, 1, 0), (1, 0, 1, 1), (0, 2, 1, 0), (3, 1, 0, 1),
-    (1, 2, 1, 0), (1, 2, 0, 1), (0, 2, 0, 1), (2, 2, 1, 0), (0, 1, 1, 1), (3, 2, 0, 1),
-    (3, 1, 1, 1), (3, 1, 1, 0), (2, 1, 1, 1), (2, 2, 0, 1), (3, 2, 1, 0), (1, 2, 1, 1),
-    (2, 1, 0, 1), (0, 2, 1, 1), (2, 2, 1, 1), (3, 0, 1, 1), (1, 1, 1, 1), (3, 2, 1, 1),
+    (0, 0, 0, 0), (1, 0, 0, 0), (0, 0, 1, 0), (2, 0, 0, 0), (3, 0, 0, 0), (1, 1, 0, 0),
+    (1, 0, 1, 0), (1, 0, 0, 1), (2, 1, 0, 0), (0, 1, 1, 0), (1, 2, 0, 0), (3, 0, 0, 1),
+    (3, 1, 0, 0), (0, 1, 0, 0), (2, 2, 0, 0), (1, 1, 0, 1), (2, 1, 0, 1), (0, 0, 0, 1),
+    (2, 0, 1, 0), (0, 2, 1, 0), (0, 1, 1, 1), (0, 0, 1, 1), (3, 0, 1, 0), (3, 2, 0, 0),
+    (1, 1, 1, 0), (1, 0, 1, 1), (0, 1, 0, 1), (3, 1, 0, 1), (0, 2, 0, 0), (1, 2, 1, 0),
+    (2, 2, 0, 1), (2, 1, 1, 0), (1, 2, 0, 1), (2, 0, 1, 1), (3, 1, 1, 0), (3, 0, 1, 1),
+    (1, 1, 1, 1), (0, 2, 1, 1), (3, 2, 0, 1), (2, 2, 1, 0), (3, 1, 1, 1), (0, 2, 0, 1),
+    (2, 0, 0, 1), (3, 2, 1, 0), (2, 1, 1, 1), (1, 2, 1, 1), (3, 2, 1, 1), (2, 2, 1, 1),
 )
 
 
@@ -369,13 +369,14 @@
 
         lax.fori_loop(0, len(batch), step, 0)
 
-    batches = [PIECES[n : n + BATCH] for n in range(0, len(PIECES), BATCH)]
+    starts = [sum(BATCHES[:b]) for b in range(len(BATCHES))]
+    batches = [PIECES[n : n + size] for n, size in zip(starts, BATCHES)]
     for b in range(len(batches) + 1):
         if b < len(batches):
             for q, piece in enumerate(batches[b]):
                 _i, _par, live = source(piece, c)
 
-                def take(n=b * BATCH + q, piece=piece):
+                def take(n=starts[b] + q, piece=piece):
                     if arrival(piece) >= 0:
                         copy_of(n, piece, 0, neighbour(up)).wait_recv()
                     for when, copy in sends_of(n, piece):

time: 102 us -> 103 us (level)
  the two profiles are of different devices: /device:TPU:128 before, /device:TPU:69 now
where the time goes in v5:
time: 103 us
  Pallas kernels  102 us (99%)
    pallas_call x1, Pallas kernels, on_device(): pl.pallas_call(kernel, out_shape=pltpu.VMEM((4, 96, 256), F32), in_specs=...  102 us

profile of v5, /device:TPU:69, one launch (start us, length us, event | category | flops | bytes accessed | tf_op | source)
XLA Modules:
  0.0 102.9 jit_solution(14659008431500736736)
XLA Ops:
  0.0 102.1 %screened.1 = f32[4,96,256]{2,1,0:T(8,128)S(1)} custom-call(f32[8]{0:T(128)} %tau.1, f32[8]{0:T(128)} %tweight.1, f32[1,32]{1,0:T(1,128)} %bitcast.9, f32[1,192]{1,0:T(1,128)} %bitcast.7, f32[1,192]{1,0:T(1,128)} %bitcast.8, f32[192,1536]{1,0:T(8,128)} %bitcast.5, f32[192,1536]{1,0:T(8,128)} %bitcast.6, f32[1536,1536]{1,0:T(8,128)} %coulomb.1), custom_call_target="tpu_custom_call" | custom-call | tf_op jit(solution)/shard_map/screened/pallas_call | solution.py:481
  102.1 0.7 copy.10
